TPU v7x, 128 devices: a whole 4x4x4 slice. The times are simulated.
128 devices in a mesh: dp: 2 (over x_hi), pipe: 4 (over z), tensor: 16 (over x_lo, y, core).
Axes of the slice: x: 4 (x_hi: 2, x_lo: 2; x = x_hi * 2 + x_lo), y: 4, z: 4, core: 2. Of those that a mesh axis runs over, the one named last changes fastest.
Arguments:
- inputs: bfloat16 [4, 3072, 8192], P('pipe', 'dp', 'tensor'), may hold values from -6 to 6
- upstream: bfloat16 [4, 3072, 8192], P('pipe', 'dp', 'tensor'), may hold values from -6 to 6
- factor_one: bfloat16 [4, 32, 4, 256, 256], P('pipe', 'tensor'), may hold values from -0.375 to 0.375
- factor_two: bfloat16 [4, 128, 256, 256], P('pipe', 'tensor'), may hold values from -0.375 to 0.375
- factor_three: bfloat16 [4, 128, 256, 256], P('pipe', 'tensor'), may hold values from -0.375 to 0.375
- factor_four: bfloat16 [4, 32, 4, 256, 256], P('pipe', 'tensor'), may hold values from -0.1875 to 0.1875
Outputs:
- y_next: bfloat16 [4, 3072, 8192], P('pipe', 'dp', 'tensor')
- dx_prev: bfloat16 [4, 3072, 8192], P('pipe', 'dp', 'tensor')
- grad_one: float32 [4, 32, 4, 256, 256], P('pipe', 'tensor')
- grad_two: float32 [4, 128, 256, 256], P('pipe', 'tensor')
- grad_three: float32 [4, 128, 256, 256], P('pipe', 'tensor')
- grad_four: float32 [4, 32, 4, 256, 256], P('pipe', 'tensor')
All inputs are finite; a program needn't handle non-finite values.
Results may differ from a plain program's by a relative error of at most 0.0068.
Values may be sent and summed in bfloat16 or wider, within the bound.
No kernel may reach another device: no remote copies, remote signals or barrier semaphores. Data moves between devices by JAX's collectives and lax.ppermute only.
A program may use at most 192 MiB of HBM per device.

v0:
```python
import jax
import jax.numpy as jnp
from jax import lax
from jax.sharding import PartitionSpec as P


def shifted(value, axis, steps):
    count = lax.axis_size(axis)
    leading, last = (max(0, -steps), min(count, count - steps))
    return lax.ppermute(value, axis, [(source, source + steps) for source in range(leading, last)])


def to_peers(blocks, parts):
    rows, local, width = blocks.shape
    inner = width // (parts * local)
    shaped = blocks.reshape(rows, local, parts, local, inner)
    return shaped.transpose(0, 2, 1, 3, 4).reshape(rows, parts, local * local * inner)


def from_peers(received, local):
    rows, parts, flat = received.shape
    inner = flat // (local * local)
    shaped = received.reshape(rows, parts, local, local, inner)
    return shaped.transpose(0, 3, 1, 2, 4).reshape(rows, local, parts * local * inner)


def shards(inputs, upstream, factor_one, factor_two, factor_three, factor_four):
    parts = lax.axis_size("tensor")
    acts = inputs[0]
    grad_out = upstream[0]
    first = factor_one[0]
    second = factor_two[0]
    third = factor_three[0]
    fourth = factor_four[0]
    groups, expand, bsize = (first.shape[0], first.shape[1], first.shape[2])
    local = groups * expand
    rows = acts.shape[0]
    grouped = acts.reshape(rows, groups, bsize)
    lifted = (
        jnp.einsum("tgi,gkij->tgkj", grouped, first, preferred_element_type=jnp.float32)
        .astype(jnp.bfloat16)
        .reshape(rows, local, bsize)
    )
    outbound = to_peers(lifted, parts)
    mixed = from_peers(
        lax.all_to_all(outbound, "tensor", split_axis=1, concat_axis=1, tiled=True), local
    )
    preact = jnp.einsum("tcj,cjn->tcn", mixed, second, preferred_element_type=jnp.float32)
    active = jax.nn.gelu(preact).astype(jnp.bfloat16)
    mixed, preact, active = (mixed, preact, active)
    narrowed = jnp.einsum("tcn,cno->tco", active, third, preferred_element_type=jnp.float32).astype(
        jnp.bfloat16
    )
    outbound = to_peers(narrowed, parts)
    spread = from_peers(
        lax.all_to_all(outbound, "tensor", split_axis=1, concat_axis=1, tiled=True), local
    )
    count = spread.shape[0]
    output = jnp.einsum(
        "tgkr,gkro->tgo",
        spread.reshape(count, groups, expand, bsize),
        fourth,
        preferred_element_type=jnp.float32,
    ).astype(jnp.bfloat16)
    spread, output = (spread, output.reshape(count, groups * bsize))
    y_next = shifted(output[None], "pipe", 1)
    grad_grouped = grad_out.reshape(rows, groups, bsize)
    spread_four = spread.reshape(rows, groups, expand, bsize)
    grad_spread = (
        jnp.einsum("tgo,gkro->tgkr", grad_grouped, fourth, preferred_element_type=jnp.float32)
        .astype(jnp.bfloat16)
        .reshape(rows, local, bsize)
    )
    grad_four = jnp.einsum(
        "tgkr,tgo->gkro", spread_four, grad_grouped, preferred_element_type=jnp.float32
    )
    outbound = to_peers(grad_spread, parts)
    grad_narrow = from_peers(
        lax.all_to_all(outbound, "tensor", split_axis=1, concat_axis=1, tiled=True), local
    )
    grad_active = jnp.einsum("tco,cno->tcn", grad_narrow, third, preferred_element_type=jnp.float32)
    grad_narrow, grad_active = (grad_narrow, grad_active)
    grad_three = jnp.einsum("tcn,tco->cno", active, grad_narrow, preferred_element_type=jnp.float32)
    pulled = jax.vjp(jax.nn.gelu, preact)[1]
    grad_pre = pulled(grad_active)[0].astype(jnp.bfloat16)
    grad_two = jnp.einsum("tcj,tcn->cjn", mixed, grad_pre, preferred_element_type=jnp.float32)
    grad_mixed = jnp.einsum(
        "tcn,cjn->tcj", grad_pre, second, preferred_element_type=jnp.float32
    ).astype(jnp.bfloat16)
    outbound = to_peers(grad_mixed, parts)
    grad_lift = from_peers(
        lax.all_to_all(outbound, "tensor", split_axis=1, concat_axis=1, tiled=True), local
    )
    count = grad_lift.shape[0]
    grad_input = jnp.einsum(
        "tgkj,gkij->tgi",
        grad_lift.reshape(count, groups, expand, bsize),
        first,
        preferred_element_type=jnp.float32,
    ).astype(jnp.bfloat16)
    grad_lift, grad_input = (grad_lift, grad_input.reshape(count, groups * bsize))
    dx_prev = shifted(grad_input[None], "pipe", -1)
    grad_one = jnp.einsum(
        "tgi,tgkj->gkij",
        grouped,
        grad_lift.reshape(rows, groups, expand, bsize),
        preferred_element_type=jnp.float32,
    )
    grad_one, grad_two, grad_three, grad_four = lax.psum(
        (grad_one, grad_two, grad_three, grad_four), "dp"
    )
    return (y_next, dx_prev, grad_one[None], grad_two[None], grad_three[None], grad_four[None])


def solution(mesh):
    return jax.shard_map(
        shards,
        mesh=mesh,
        in_specs=(
            P("pipe", "dp", "tensor"),
            P("pipe", "dp", "tensor"),
            P("pipe", "tensor", None, None, None),
            P("pipe", "tensor", None, None),
            P("pipe", "tensor", None, None),
            P("pipe", "tensor", None, None, None),
        ),
        out_specs=(
            P("pipe", "dp", "tensor"),
            P("pipe", "dp", "tensor"),
            P("pipe", "tensor", None, None, None),
            P("pipe", "tensor", None, None),
            P("pipe", "tensor", None, None),
            P("pipe", "tensor", None, None, None),
        ),
        check_vma=False,
    )
```

profile of v0, /device:TPU:1, one launch (start us, length us, event | category | flops | bytes accessed | tf_op | source)
XLA Modules:
  0.0 716.7 jit_solution(1809731829033732592)
XLA Ops:
  9.7 6.5 convert_bitcast_fusion.3
  16.1 13.6 %reshape_reshape.14 = bf16[1536,8,16,8,2]{0,4,3,2,1:T(2,128)(2,1)} reshape(bf16[1536,2,4,256]{0,3,2,1:T(8,128)(2,1)} %convert_bitcast_fusion.3) | data formatting | bytes 12582912 | tf_op jit(solution)/shard_map/reshape;reshape | solution.py:16
  29.7 9.5 %copy.53 = bf16[1536,8,16,8,2]{0,2,4,3,1:T(8,128)(2,1)S(1)} copy(bf16[1536,8,16,8,2]{0,4,3,2,1:T(2,128)(2,1)} %reshape_reshape.14) | data formatting | bytes 12582912 | tf_op jit(solution)/shard_map/reshape;reshape | solution.py:16
  45.3 7.2 %all-to-all-start = ((bf16[1536,16,128]{0,2,1:T(8,128)(2,1)}), bf16[1536,16,128]{0,2,1:T(8,128)(2,1)}, u32[]{:S(2)}, u32[]{:S(2)}) async-start(bf16[1536,16,128]{0,2,1:T(8,128)(2,1)} %copy.54), calls=%async_computation | async-start | bytes 12582912 | tf_op jit(solution)/shard_map/all_to_all | solution.py:46
  61.2 13.1 %reshape_reshape.16 = bf16[1536,8,16,8,2]{0,4,3,2,1:T(2,128)(2,1)} reshape(bf16[1536,2,4,256]{0,3,2,1:T(8,128)(2,1)} %convert_bitcast_fusion.1) | data formatting | bytes 12582912 | tf_op jit(solution)/shard_map/reshape;reshape | solution.py:16
  74.3 9.5 %copy.67 = bf16[1536,8,16,8,2]{0,2,4,3,1:T(8,128)(2,1)S(1)} copy(bf16[1536,8,16,8,2]{0,4,3,2,1:T(2,128)(2,1)} %reshape_reshape.16) | data formatting | bytes 12582912 | tf_op jit(solution)/shard_map/reshape;reshape | solution.py:16
  89.9 51.1 %all-to-all-done = bf16[1536,16,128]{0,2,1:T(8,128)(2,1)} async-done(((bf16[1536,16,128]{0,2,1:T(8,128)(2,1)}), bf16[1536,16,128]{0,2,1:T(8,128)(2,1)}, u32[]{:S(2)}, u32[]{:S(2)}) %all-to-all-start) | async-done | bytes 6291488 | tf_op jit(solution)/shard_map/all_to_all | solution.py:46
  141.0 12.3 %all-to-all-start.2 = ((bf16[1536,16,128]{0,2,1:T(8,128)(2,1)}), bf16[1536,16,128]{0,2,1:T(8,128)(2,1)}, u32[]{:S(2)}, u32[]{:S(2)}) async-start(bf16[1536,16,128]{0,2,1:T(8,128)(2,1)} %copy.68), calls=%async_computation.2 | async-start | bytes 12582912 | tf_op jit(solution)/shard_map/all_to_all | solution.py:79
  153.3 6.3 copy.55
  163.1 9.2 %fusion.11 = f32[8,1536,256]{2,1,0:T(8,128)} fusion(bf16[1536,8,256]{0,1,2:T(8,128)(2,1)S(1)} %bitcast.136, bf16[1,8,256,256]{3,2,1,0:T(8,128)(2,1)S(1)} %copy-done.3), kind=kOutput, calls=%fused_computation.20 | convolution fusion | flops 1610612736 | bytes 19922944 | tf_op jit(solution)/shard_map/tcj,cjn->tcn/dot_general | solution.py:48
  172.3 9.7 %convert_bitcast_fusion.2 = bf16[1536,8,256]{0,2,1:T(8,128)(2,1)} fusion(bf16[1,8,256,256]{3,2,1,0:T(8,128)(2,1)S(1)} %copy-done, f32[8,1536,256]{2,1,0:T(8,128)} %fusion.11), kind=kOutput, calls=%fused_computation.18 | convolution fusion | flops 1642070016 | bytes 19922944 | tf_op jit(solution)/shard_map/tcn,cno->tco/dot_general | solution.py:51
  182.0 13.1 %reshape.51 = bf16[1536,8,16,8,2]{0,4,3,2,1:T(2,128)(2,1)} reshape(bf16[1536,8,256]{0,2,1:T(8,128)(2,1)} %convert_bitcast_fusion.2) | data formatting | bytes 12582912 | tf_op jit(solution)/shard_map/reshape | solution.py:16
  195.1 9.5 %copy.59 = bf16[1536,8,16,8,2]{0,2,4,3,1:T(8,128)(2,1)S(1)} copy(bf16[1536,8,16,8,2]{0,4,3,2,1:T(2,128)(2,1)} %reshape.51) | data formatting | bytes 12582912 | tf_op jit(solution)/shard_map/reshape | solution.py:16
  210.8 30.9 %all-to-all-done.2 = bf16[1536,16,128]{0,2,1:T(8,128)(2,1)} async-done(((bf16[1536,16,128]{0,2,1:T(8,128)(2,1)}), bf16[1536,16,128]{0,2,1:T(8,128)(2,1)}, u32[]{:S(2)}, u32[]{:S(2)}) %all-to-all-start.2) | async-done | bytes 6291488 | tf_op jit(solution)/shard_map/all_to_all | solution.py:79
  241.7 12.1 %all-to-all-start.1 = ((bf16[1536,16,128]{0,2,1:T(8,128)(2,1)}), bf16[1536,16,128]{0,2,1:T(8,128)(2,1)}, u32[]{:S(2)}, u32[]{:S(2)}) async-start(bf16[1536,16,128]{0,2,1:T(8,128)(2,1)} %copy.60), calls=%async_computation.1 | async-start | bytes 12582912 | tf_op jit(solution)/shard_map/all_to_all | solution.py:56
  253.8 6.3 copy.69
  266.2 9.1 %copy.71 = bf16[1536,8,256]{2,0,1:T(8,128)(2,1)} copy(bf16[1536,8,256]{0,1,2:T(8,128)(2,1)} %bitcast.143) | data formatting | bytes 12582912 | tf_op jit(solution)/shard_map/reshape | solution.py:24
  275.3 14.1 %fusion.6 = bf16[1536,8,256]{2,0,1:T(8,128)(2,1)S(1)} fusion(f32[8,1536,256]{2,1,0:T(8,128)} %fusion.11, bf16[1536,8,256]{2,0,1:T(8,128)(2,1)} %copy.71, bf16[1,8,256,256]{3,2,1,0:T(8,128)(2,1)S(1)} %copy-done), kind=kOutput, calls=%fused_computation.8 | convolution fusion | flops 1673527296 | bytes 26214400 | tf_op jit(solution)/shard_map/tco,cno->tcn/dot_general | solution.py:81
  296.4 13.3 %reshape.57 = bf16[1536,8,16,8,2]{0,4,3,2,1:T(2,128)(2,1)} reshape(bf16[1536,8,256]{0,2,1:T(8,128)(2,1)} %convert_bitcast_fusion) | data formatting | bytes 12582912 | tf_op jit(solution)/shard_map/reshape | solution.py:16
  309.7 9.5 %copy.72 = bf16[1536,8,16,8,2]{0,2,4,3,1:T(8,128)(2,1)S(1)} copy(bf16[1536,8,16,8,2]{0,4,3,2,1:T(2,128)(2,1)} %reshape.57) | data formatting | bytes 12582912 | tf_op jit(solution)/shard_map/reshape | solution.py:16
  325.3 16.9 %all-to-all-done.1 = bf16[1536,16,128]{0,2,1:T(8,128)(2,1)} async-done(((bf16[1536,16,128]{0,2,1:T(8,128)(2,1)}), bf16[1536,16,128]{0,2,1:T(8,128)(2,1)}, u32[]{:S(2)}, u32[]{:S(2)}) %all-to-all-start.1) | async-done | bytes 6291488 | tf_op jit(solution)/shard_map/all_to_all | solution.py:56
  342.2 11.7 %all-to-all-start.3 = ((bf16[1536,16,128]{0,2,1:T(8,128)(2,1)}), bf16[1536,16,128]{0,2,1:T(8,128)(2,1)}, u32[]{:S(2)}, u32[]{:S(2)}) async-start(bf16[1536,16,128]{0,2,1:T(8,128)(2,1)} %copy.73), calls=%async_computation.3 | async-start | bytes 12582912 | tf_op jit(solution)/shard_map/all_to_all | solution.py:92
  354.2 8.2 %fusion.17 = f32[1,8,256,256]{3,2,1,0:T(8,128)} fusion(bf16[1536,8,256]{2,0,1:T(8,128)(2,1)} %copy-done.4, bf16[1536,8,256]{0,1,2:T(8,128)(2,1)} %bitcast.137), kind=kOutput, calls=%fused_computation.28 | convolution fusion | flops 1610612736 | bytes 14680064 | tf_op jit(solution)/shard_map/tcj,tcn->cjn/dot_general | solution.py:86
  362.4 12.5 %convolution_bitcast_fusion.3 = f32[1,8,256,256]{3,2,1,0:T(8,128)} fusion(bf16[1536,8,256]{2,0,1:T(8,128)(2,1)} %copy.71, f32[8,1536,256]{2,1,0:T(8,128)} %fusion.11), kind=kOutput, calls=%fused_computation.30 | convolution fusion | flops 1638924288 | bytes 20971520 | tf_op jit(solution)/shard_map/tcn,tco->cno/dot_general | solution.py:83
  381.2 7.4 %copy.62 = bf16[1536,8,16,8,2]{0,4,3,2,1:T(2,128)(2,1)} copy(bf16[1536,8,16,8,2]{0,2,4,1,3:T(8,128)(2,1)S(1)} %bitcast.145) | data formatting | bytes 12582912 | tf_op jit(solution)/shard_map/transpose | solution.py:24
  388.7 13.6 %reshape_reshape.15 = bf16[1536,2,4,256]{0,3,2,1:T(8,128)(2,1)} reshape(bf16[1536,8,16,8,2]{0,4,3,2,1:T(2,128)(2,1)} %copy.62) | data formatting | bytes 12582912 | tf_op jit(solution)/shard_map/reshape;reshape | solution.py:61
  402.3 40.2 %all-to-all-done.3 = bf16[1536,16,128]{0,2,1:T(8,128)(2,1)} async-done(((bf16[1536,16,128]{0,2,1:T(8,128)(2,1)}), bf16[1536,16,128]{0,2,1:T(8,128)(2,1)}, u32[]{:S(2)}, u32[]{:S(2)}) %all-to-all-start.3) | async-done | bytes 6291488 | tf_op jit(solution)/shard_map/all_to_all | solution.py:92
  448.8 7.1 copy.75
  455.9 13.7 %reshape_reshape.17 = bf16[1536,2,4,256]{0,3,2,1:T(8,128)(2,1)} reshape(bf16[1536,8,16,8,2]{0,4,3,2,1:T(2,128)(2,1)} %copy.75) | data formatting | bytes 12582912 | tf_op jit(solution)/shard_map/reshape;reshape | solution.py:97
  502.8 22.9 %collective-permute-done = bf16[1,1536,512]{2,1,0:T(8,128)(2,1)S(1)} collective-permute-done((bf16[1,1536,512]{2,1,0:T(8,128)(2,1)}, bf16[1,1536,512]{2,1,0:T(8,128)(2,1)S(1)}, u32[]{:S(2)}, u32[]{:S(2)}) %collective-permute-start) | collective-permute-done | bytes 1572896 | tf_op jit(solution)/shard_map/ppermute | solution.py:10
  525.6 13.1 %collective-permute-done.1 = bf16[1,1536,512]{2,1,0:T(8,128)(2,1)} collective-permute-done((bf16[1,1536,512]{2,1,0:T(8,128)(2,1)}, bf16[1,1536,512]{2,1,0:T(8,128)(2,1)}, u32[]{:S(2)}, u32[]{:S(2)}) %collective-permute-start.1) | collective-permute-done | bytes 1572896 | tf_op jit(solution)/shard_map/ppermute | solution.py:10
  538.7 158.1 %all-reduce.3.cloned.1.call-done = (f32[1,2,4,256,256]{3,4,2,1,0:T(8,128)}, f32[1,8,256,256]{3,2,1,0:T(8,128)}, f32[1,8,256,256]{3,2,1,0:T(8,128)}, f32[1,2,4,256,256]{4,3,2,1,0:T(8,128)}) async-done(((f32[1,2,4,256,256]{3,4,2,1,0:T(8,128)}, f32[1,8,256,256]{3,2,1,0:T(8,128)}, f32[1,8,256,256]{3,2,1,0:T(8,128)}, f32[1,2,4,256,256]{4,3,2,1,0:T(8,128)}), (f32[1,2,4,256,256]{3,4,2,1,0:T(8,128)}, ...) | async-done | bytes 8388624 | tf_op jit(solution)/shard_map/psum | solution.py:109
  (56 shorter events, 110.8 us)
Async XLA Ops:
  7.2 165.1 %copy-start = (bf16[1,8,256,256]{3,2,1,0:T(8,128)(2,1)S(1)}, bf16[1,8,256,256]{3,2,1,0:T(8,128)(2,1)}, u32[]{:S(2)}) copy-start(bf16[1,8,256,256]{3,2,1,0:T(8,128)(2,1)} %param.10) | copy-start | bytes 3145732
  9.6 20.1 %copy-start.5 = (bf16[1536,2,256]{2,1,0:T(2,128)(2,1)}, bf16[1536,2,256]{2,1,0:T(2,128)(2,1)S(1)}, u32[]{:S(2)}) copy-start(bf16[1536,2,256]{2,1,0:T(2,128)(2,1)S(1)} %reshape_squeeze.6) | copy-start | bytes 4718596
  45.3 95.7 %all-to-all-start = ((bf16[1536,16,128]{0,2,1:T(8,128)(2,1)}), bf16[1536,16,128]{0,2,1:T(8,128)(2,1)}, u32[]{:S(2)}, u32[]{:S(2)}) async-start(bf16[1536,16,128]{0,2,1:T(8,128)(2,1)} %copy.54), calls=%async_computation | async-start | bytes 12582912 | tf_op jit(solution)/shard_map/all_to_all | solution.py:46
  54.9 19.4 %copy-start.7 = (bf16[1536,2,256]{2,1,0:T(2,128)(2,1)}, bf16[1536,2,256]{2,1,0:T(2,128)(2,1)S(1)}, u32[]{:S(2)}) copy-start(bf16[1536,2,256]{2,1,0:T(2,128)(2,1)S(1)} %reshape_squeeze.7) | copy-start | bytes 4718596
  141.0 100.7 %all-to-all-start.2 = ((bf16[1536,16,128]{0,2,1:T(8,128)(2,1)}), bf16[1536,16,128]{0,2,1:T(8,128)(2,1)}, u32[]{:S(2)}, u32[]{:S(2)}) async-start(bf16[1536,16,128]{0,2,1:T(8,128)(2,1)} %copy.68), calls=%async_computation.2 | async-start | bytes 12582912 | tf_op jit(solution)/shard_map/all_to_all | solution.py:79
  159.5 3.5 copy-start.3
  163.0 9.3 %copy-start.2 = (bf16[1536,8,16,8,2]{0,1,4,3,2:T(8,128)(2,1)}, bf16[1536,8,16,8,2]{0,1,4,3,2:T(8,128)(2,1)S(1)}, u32[]{:S(2)}) copy-start(bf16[1536,8,16,8,2]{0,1,4,3,2:T(8,128)(2,1)S(1)} %copy.56) | copy-start | bytes 18874372
  241.7 100.5 %all-to-all-start.1 = ((bf16[1536,16,128]{0,2,1:T(8,128)(2,1)}), bf16[1536,16,128]{0,2,1:T(8,128)(2,1)}, u32[]{:S(2)}, u32[]{:S(2)}) async-start(bf16[1536,16,128]{0,2,1:T(8,128)(2,1)} %copy.60), calls=%async_computation.1 | async-start | bytes 12582912 | tf_op jit(solution)/shard_map/all_to_all | solution.py:56
  289.4 2.6 copy-start.4
  342.2 100.3 %all-to-all-start.3 = ((bf16[1536,16,128]{0,2,1:T(8,128)(2,1)}), bf16[1536,16,128]{0,2,1:T(8,128)(2,1)}, u32[]{:S(2)}, u32[]{:S(2)}) async-start(bf16[1536,16,128]{0,2,1:T(8,128)(2,1)} %copy.73), calls=%async_computation.3 | async-start | bytes 12582912 | tf_op jit(solution)/shard_map/all_to_all | solution.py:92
  354.0 342.9 %all-reduce.3.cloned.1.call-start = ((), (), s32[]{:S(2)}) async-start(), calls=%async_computation.4 | async-start | bytes 16777216 | tf_op jit(solution)/shard_map/psum | solution.py:109
  455.9 13.7 %copy-start.6 = (bf16[1536,2,256]{2,1,0:T(2,128)(2,1)S(1)}, bf16[1536,2,256]{2,1,0:T(2,128)(2,1)}, u32[]{:S(2)}) copy-start(bf16[1536,2,256]{2,1,0:T(2,128)(2,1)} %copy-done.5) | copy-start | bytes 4718596
  469.6 6.0 copy-start.8
  481.5 1.2 copy-start.13
  489.0 36.7 %collective-permute-start = (bf16[1,1536,512]{2,1,0:T(8,128)(2,1)}, bf16[1,1536,512]{2,1,0:T(8,128)(2,1)S(1)}, u32[]{:S(2)}, u32[]{:S(2)}) collective-permute-start(bf16[1,1536,512]{2,1,0:T(8,128)(2,1)} %copy.65), channel_id=1, source_target_pairs={{0,16},{16,32},{32,48},{1,17},{17,33},{33,49},{2,18},{18,34},{34,5... | collective-permute-start | bytes 4718600 | tf_op jit(solution)/shard_map/ppermute | solution.py:10
  501.5 37.3 %collective-permute-start.1 = (bf16[1,1536,512]{2,1,0:T(8,128)(2,1)}, bf16[1,1536,512]{2,1,0:T(8,128)(2,1)}, u32[]{:S(2)}, u32[]{:S(2)}) collective-permute-start(bf16[1,1536,512]{2,1,0:T(8,128)(2,1)} %copy.77), channel_id=1, source_target_pairs={{16,0},{32,16},{48,32},{17,1},{33,17},{49,33},{18,2},{34,18},{50,3... | collective-permute-start | bytes 4718600 | tf_op jit(solution)/shard_map/ppermute | solution.py:10
  525.6 13.1 %copy-start.12 = (bf16[1,1536,512]{2,1,0:T(8,128)(2,1)}, bf16[1,1536,512]{2,1,0:T(8,128)(2,1)S(1)}, u32[]{:S(2)}) copy-start(bf16[1,1536,512]{2,1,0:T(8,128)(2,1)S(1)} %collective-permute-done) | copy-start | bytes 4718596
  696.8 8.6 %copy-start.11 = (f32[1,8,256,256]{3,2,1,0:T(8,128)S(1)}, f32[1,8,256,256]{3,2,1,0:T(8,128)}, u32[]{:S(2)}) copy-start(f32[1,8,256,256]{3,2,1,0:T(8,128)} %get-tuple-element.37) | copy-start | bytes 6291460
  699.9 6.9 copy-start.10
  702.7 5.5 copy-start.9
  702.7 6.8 copy-start.1
Sparse Core Ops, SparseCore 0:
  481.7 215.1 all-reduce.2
where the time goes:
time: 723 us; the launch traced here: 717 us
  waiting for transfers between devices  333 us (46%)
  local copies, waits for them, and re-layouts  227 us (31%)
  matrix products  93.5 us (13%)
  starting transfers between devices  48.5 us (7%)
  between operations  14.7 us (2%)
    psum x1, waiting for transfers between devices, shards(): lax.psum((grad_one, grad_two, grad_three, grad_four), 'dp')  158 us
    all_to_all x4, waiting for transfers between devices, shards(): lax.all_to_all(outbound, 'tensor', split_axis=1, concat_axis=1, tiled=True)  139 us
    another operation x4, local copies, waits for them, and re-layouts, to_peers(): shaped = blocks.reshape(rows, local, parts, local, inner)  45.6 us
    reshape x4, local copies, waits for them, and re-layouts, to_peers(): shaped = blocks.reshape(rows, local, parts, local, inner)  45.3 us
    all_to_all x4, starting transfers between devices, shards(): lax.all_to_all(outbound, 'tensor', split_axis=1, concat_axis=1, tiled=True)  43.3 us
    ppermute x2, waiting for transfers between devices, shifted(): lax.ppermute(value, axis, [(source, source + steps) for source in range(l...  36 us
    all_to_all x4, local copies, waits for them, and re-layouts, shards(): lax.all_to_all(outbound, 'tensor', split_axis=1, concat_axis=1, tiled=True)  25 us
    reshape x4, local copies, waits for them, and re-layouts, to_peers(): shaped.transpose(0, 2, 1, 3, 4).reshape(rows, parts, local * local * inner)  24.6 us
  transfers between devices with their start and end apart: 7, of which 7 were waited for; matrix products, arithmetic and copies ran while one was open for 32% of the time, Pallas kernels for 0%

commit v1 on v0

--- a/solution.py
+++ b/solution.py
@@ -2,6 +2,13 @@
 import jax.numpy as jnp
 from jax import lax
 from jax.sharding import PartitionSpec as P
+
+
+def swap_blocks(x, mesh_axis, split, join):
+    size = lax.axis_size(mesh_axis)
+    blocks = jnp.stack(jnp.split(x, size, axis=split), axis=0)
+    blocks = lax.all_to_all(blocks, mesh_axis, split_axis=0, concat_axis=0)
+    return jnp.concatenate(blocks, axis=join)
 
 
 def shifted(value, axis, steps):
@@ -88,9 +95,7 @@
         "tcn,cjn->tcj", grad_pre, second, preferred_element_type=jnp.float32
     ).astype(jnp.bfloat16)
     outbound = to_peers(grad_mixed, parts)
-    grad_lift = from_peers(
-        lax.all_to_all(outbound, "tensor", split_axis=1, concat_axis=1, tiled=True), local
-    )
+    grad_lift = from_peers(swap_blocks(outbound, "tensor", 1, 1), local)
     count = grad_lift.shape[0]
     grad_input = jnp.einsum(
         "tgkj,gkij->tgi",

time: 723 us -> 829 us (1.15)
  local copies, waits for them, and re-layouts: 227 us -> 318 us
  waiting for transfers between devices: 333 us -> 346 us
    split x0 -> x17, local copies, waits for them, and re-layouts: none -> 65.2 us  [swap_blocks(): blocks = jnp.stack(jnp.split(x, size, axis=split), axis=0)]
    all_to_all x0 -> x1, waiting for transfers between devices: none -> 34.2 us  [swap_blocks(): blocks = lax.all_to_all(blocks, mesh_axis, split_axis=0, concat_axis=0)]
    all_to_all x4 -> x3, waiting for transfers between devices: 139 us -> 118 us  [shards(): lax.all_to_all(outbound, 'tensor', split_axis=1, concat_axis=1, tiled=True)]
    unnamed x34 -> x59, local copies, waits for them, and re-layouts: 16.4 us -> 36.6 us
    all_to_all x4 -> x3, starting transfers between devices: 43.3 us -> 31.6 us  [shards(): lax.all_to_all(outbound, 'tensor', split_axis=1, concat_axis=1, tiled=True)]
    all_to_all x0 -> x1, starting transfers between devices: none -> 11.4 us  [swap_blocks(): blocks = lax.all_to_all(blocks, mesh_axis, split_axis=0, concat_axis=0)]
    reshape x0 -> x1, local copies, waits for them, and re-layouts: none -> 9.06 us  [swap_blocks(): return jnp.concatenate(blocks, axis=join)]
    reshape x4 -> x3, local copies, waits for them, and re-layouts: 24.6 us -> 18.3 us  [to_peers(): shaped.transpose(0, 2, 1, 3, 4).reshape(rows, parts, local * local * inner)]
  transfers between devices with their start and end apart: 7 -> 7, of which waited for: 7 -> 6; matrix products, arithmetic and copies ran while one was open for 32% -> 26% of each run, Pallas kernels for 0% -> 0%
where the time goes in v1:
time: 829 us; the launch traced here: 822 us
  waiting for transfers between devices  346 us (42%)
  local copies, waits for them, and re-layouts  318 us (38%)
  matrix products  94.8 us (11%)
  starting transfers between devices  48.4 us (6%)
  between operations  14.5 us (2%)
    psum x1, waiting for transfers between devices, shards(): lax.psum((grad_one, grad_two, grad_three, grad_four), 'dp')  158 us
    all_to_all x3, waiting for transfers between devices, shards(): lax.all_to_all(outbound, 'tensor', split_axis=1, concat_axis=1, tiled=True)  118 us
    split x17, local copies, waits for them, and re-layouts, swap_blocks(): blocks = jnp.stack(jnp.split(x, size, axis=split), axis=0)  65.2 us
    reshape x4, local copies, waits for them, and re-layouts, to_peers(): shaped = blocks.reshape(rows, local, parts, local, inner)  48.3 us
    another operation x4, local copies, waits for them, and re-layouts, to_peers(): shaped = blocks.reshape(rows, local, parts, local, inner)  45.3 us
    unnamed x59, local copies, waits for them, and re-layouts  36.6 us
    ppermute x2, waiting for transfers between devices, shifted(): lax.ppermute(value, axis, [(source, source + steps) for source in range(l...  36 us
    all_to_all x1, waiting for transfers between devices, swap_blocks(): blocks = lax.all_to_all(blocks, mesh_axis, split_axis=0, concat_axis=0)  34.2 us
  transfers between devices with their start and end apart: 7, of which 6 were waited for; matrix products, arithmetic and copies ran while one was open for 26% of the time, Pallas kernels for 0%

profile of v1, /device:TPU:1, one launch (start us, length us, event | category | flops | bytes accessed | tf_op | source)
XLA Modules:
  0.0 821.5 jit_solution(12262878906491480694)
XLA Ops:
  15.9 13.3 %reshape_reshape.19 = bf16[1536,8,16,8,2]{0,4,3,2,1:T(2,128)(2,1)} reshape(bf16[1536,2,4,256]{0,3,2,1:T(8,128)(2,1)} %convert_bitcast_fusion.1) | data formatting | bytes 12582912 | tf_op jit(solution)/shard_map/reshape;reshape | solution.py:23
  29.2 9.5 %copy.834 = bf16[1536,8,16,8,2]{0,2,4,3,1:T(8,128)(2,1)S(1)} copy(bf16[1536,8,16,8,2]{0,4,3,2,1:T(2,128)(2,1)} %reshape_reshape.19) | data formatting | bytes 12582912 | tf_op jit(solution)/shard_map/reshape;reshape | solution.py:23
  44.8 7.3 all-to-all-start.2
  54.4 6.5 convert_bitcast_fusion.3
  60.9 13.1 %reshape_reshape.17 = bf16[1536,8,16,8,2]{0,4,3,2,1:T(2,128)(2,1)} reshape(bf16[1536,2,4,256]{0,3,2,1:T(8,128)(2,1)} %convert_bitcast_fusion.3) | data formatting | bytes 12582912 | tf_op jit(solution)/shard_map/reshape;reshape | solution.py:23
  74.0 9.5 %copy.820 = bf16[1536,8,16,8,2]{0,2,4,3,1:T(8,128)(2,1)S(1)} copy(bf16[1536,8,16,8,2]{0,4,3,2,1:T(2,128)(2,1)} %reshape_reshape.17) | data formatting | bytes 12582912 | tf_op jit(solution)/shard_map/reshape;reshape | solution.py:23
  89.6 50.9 %all-to-all-done.2 = bf16[1536,16,128]{0,2,1:T(8,128)(2,1)} async-done(((bf16[1536,16,128]{0,2,1:T(8,128)(2,1)}), bf16[1536,16,128]{0,2,1:T(8,128)(2,1)}, u32[]{:S(2)}, u32[]{:S(2)}) %all-to-all-start.2) | async-done | bytes 6291488 | tf_op jit(solution)/shard_map/all_to_all | solution.py:86
  140.5 12.3 %all-to-all-start = ((bf16[1536,16,128]{0,2,1:T(8,128)(2,1)}), bf16[1536,16,128]{0,2,1:T(8,128)(2,1)}, u32[]{:S(2)}, u32[]{:S(2)}) async-start(bf16[1536,16,128]{0,2,1:T(8,128)(2,1)} %copy.821), calls=%async_computation | async-start | bytes 12582912 | tf_op jit(solution)/shard_map/all_to_all | solution.py:53
  165.1 9.3 %copy.838 = bf16[1536,8,256]{2,0,1:T(8,128)(2,1)} copy(bf16[1536,8,256]{0,1,2:T(8,128)(2,1)} %bitcast.175) | data formatting | bytes 12582912 | tf_op jit(solution)/shard_map/reshape | solution.py:31
  174.4 66.8 %all-to-all-done = bf16[1536,16,128]{0,2,1:T(8,128)(2,1)} async-done(((bf16[1536,16,128]{0,2,1:T(8,128)(2,1)}), bf16[1536,16,128]{0,2,1:T(8,128)(2,1)}, u32[]{:S(2)}, u32[]{:S(2)}) %all-to-all-start) | async-done | bytes 6291488 | tf_op jit(solution)/shard_map/all_to_all | solution.py:53
  251.0 9.2 %fusion.11 = f32[8,1536,256]{2,1,0:T(8,128)} fusion(bf16[1536,8,256]{0,1,2:T(8,128)(2,1)S(1)} %bitcast.170, bf16[1,8,256,256]{3,2,1,0:T(8,128)(2,1)S(1)} %copy-done.3), kind=kOutput, calls=%fused_computation.20 | convolution fusion | flops 1610612736 | bytes 19922944 | tf_op jit(solution)/shard_map/tcj,cjn->tcn/dot_general | solution.py:55
  260.2 9.9 %convert_bitcast_fusion.2 = bf16[1536,8,256]{0,2,1:T(8,128)(2,1)} fusion(bf16[1,8,256,256]{3,2,1,0:T(8,128)(2,1)S(1)} %copy-done, f32[8,1536,256]{2,1,0:T(8,128)} %fusion.11), kind=kOutput, calls=%fused_computation.18 | convolution fusion | flops 1642070016 | bytes 19922944 | tf_op jit(solution)/shard_map/tcn,cno->tco/dot_general | solution.py:58
  270.1 12.6 %fusion.6 = bf16[1536,8,256]{2,0,1:T(8,128)(2,1)} fusion(f32[8,1536,256]{2,1,0:T(8,128)} %fusion.11, bf16[1536,8,256]{2,0,1:T(8,128)(2,1)S(1)} %bitcast.181, bf16[1,8,256,256]{3,2,1,0:T(8,128)(2,1)S(1)} %copy-done), kind=kOutput, calls=%fused_computation.8 | convolution fusion | flops 1673527296 | bytes 26214400 | tf_op jit(solution)/shard_map/tco,cno->tcn/dot_general | solution.py:88
  282.7 7.2 convert_bitcast_fusion
  290.0 13.5 %reshape.57 = bf16[1536,8,16,8,2]{0,4,3,2,1:T(2,128)(2,1)} reshape(bf16[1536,8,256]{0,2,1:T(8,128)(2,1)} %convert_bitcast_fusion) | data formatting | bytes 12582912 | tf_op jit(solution)/shard_map/reshape | solution.py:23
  303.5 12.1 %copy.839 = bf16[1536,8,16,8,2]{0,2,4,3,1:T(8,128)(2,1)} copy(bf16[1536,8,16,8,2]{0,4,3,2,1:T(2,128)(2,1)} %reshape.57) | data formatting | bytes 12582912 | tf_op jit(solution)/shard_map/reshape | solution.py:23
  315.5 13.3 %reshape.51 = bf16[1536,8,16,8,2]{0,4,3,2,1:T(2,128)(2,1)} reshape(bf16[1536,8,256]{0,2,1:T(8,128)(2,1)} %convert_bitcast_fusion.2) | data formatting | bytes 12582912 | tf_op jit(solution)/shard_map/reshape | solution.py:23
  328.8 9.5 %copy.826 = bf16[1536,8,16,8,2]{0,2,4,3,1:T(8,128)(2,1)S(1)} copy(bf16[1536,8,16,8,2]{0,4,3,2,1:T(2,128)(2,1)} %reshape.51) | data formatting | bytes 12582912 | tf_op jit(solution)/shard_map/reshape | solution.py:23
  344.4 12.1 %all-to-all-start.1 = ((bf16[1536,16,128]{0,2,1:T(8,128)(2,1)}), bf16[1536,16,128]{0,2,1:T(8,128)(2,1)}, u32[]{:S(2)}, u32[]{:S(2)}) async-start(bf16[1536,16,128]{0,2,1:T(8,128)(2,1)} %copy.827), calls=%async_computation.1 | async-start | bytes 12582912 | tf_op jit(solution)/shard_map/all_to_all | solution.py:63
  356.5 24.9 %fusion.34 = (bf16[1536,1,128]{0,1,2:T(2,128)(2,1)}, bf16[1536,1,128]{0,1,2:T(2,128)(2,1)}, bf16[1536,1,128]{0,1,2:T(2,128)(2,1)}, bf16[1536,1,128]{0,1,2:T(2,12...) fusion(bf16[1536,16,128]{0,1,2:T(8,128)(2,1)} %bitcast.169), kind=kLoop, calls=%fused_computation.60 | loop fusion | bytes 12582912 | tf_op jit(solution)/shard_map/split | solution.py:9
  445.2 11.4 %all-to-all-start.3 = ((bf16[16,1536,1,128]{3,1,2,0:T(8,128)(2,1)}), bf16[16,1536,1,128]{3,1,2,0:T(8,128)(2,1)}, u32[]{:S(2)}, u32[]{:S(2)}) async-start(bf16[16,1536,1,128]{3,1,2,0:T(8,128)(2,1)} %bitcast_dynamic-update-slice_fusion), calls=%async_computation.3 | async-start | bytes 12582912 | tf_op jit(solution)/shard_map/all_to_all | solution.py:10
  457.1 8.2 %fusion.17 = f32[1,8,256,256]{3,2,1,0:T(8,128)} fusion(bf16[1536,8,256]{2,0,1:T(8,128)(2,1)} %fusion.6, bf16[1536,8,256]{0,1,2:T(8,128)(2,1)} %bitcast.171), kind=kOutput, calls=%fused_computation.28 | convolution fusion | flops 1610612736 | bytes 14680064 | tf_op jit(solution)/shard_map/tcj,tcn->cjn/dot_general | solution.py:93
  465.3 12.4 %convolution_bitcast_fusion.3 = f32[1,8,256,256]{3,2,1,0:T(8,128)} fusion(bf16[1536,8,256]{2,0,1:T(8,128)(2,1)} %copy.838, f32[8,1536,256]{2,1,0:T(8,128)} %fusion.11), kind=kOutput, calls=%fused_computation.30 | convolution fusion | flops 1638924288 | bytes 20971520 | tf_op jit(solution)/shard_map/tcn,tco->cno/dot_general | solution.py:90
  484.0 7.3 copy.829
  491.3 13.7 %reshape_reshape.18 = bf16[1536,2,4,256]{0,3,2,1:T(8,128)(2,1)} reshape(bf16[1536,8,16,8,2]{0,4,3,2,1:T(2,128)(2,1)} %copy.829) | data formatting | bytes 12582912 | tf_op jit(solution)/shard_map/reshape;reshape | solution.py:68
  511.0 34.2 %all-to-all-done.3 = bf16[16,1536,1,128]{3,1,2,0:T(8,128)(2,1)} async-done(((bf16[16,1536,1,128]{3,1,2,0:T(8,128)(2,1)}), bf16[16,1536,1,128]{3,1,2,0:T(8,128)(2,1)}, u32[]{:S(2)}, u32[]{:S(2)}) %all-to-all-start.3) | async-done | bytes 6291488 | tf_op jit(solution)/shard_map/all_to_all | solution.py:10
  545.2 9.1 %copy.856 = bf16[1536,16,1,128]{0,1,3,2:T(8,128)(2,1)} copy(bf16[1536,16,1,128]{3,0,2,1:T(8,128)(2,1)} %bitcast.49) | data formatting | bytes 12582912 | tf_op jit(solution)/shard_map/reshape | solution.py:11
  554.2 12.7 %copy.857 = bf16[1536,8,16,8,2]{0,4,3,2,1:T(2,128)(2,1)} copy(bf16[1536,8,16,8,2]{0,2,4,1,3:T(8,128)(2,1)} %bitcast.179) | data formatting | bytes 12582912 | tf_op jit(solution)/shard_map/transpose | solution.py:31
  566.9 13.7 %reshape_reshape.21 = bf16[1536,2,4,256]{0,3,2,1:T(8,128)(2,1)} reshape(bf16[1536,8,16,8,2]{0,4,3,2,1:T(2,128)(2,1)} %copy.857) | data formatting | bytes 12582912 | tf_op jit(solution)/shard_map/reshape;reshape | solution.py:102
  607.8 22.9 %collective-permute-done = bf16[1,1536,512]{2,1,0:T(8,128)(2,1)S(1)} collective-permute-done((bf16[1,1536,512]{2,1,0:T(8,128)(2,1)}, bf16[1,1536,512]{2,1,0:T(8,128)(2,1)S(1)}, u32[]{:S(2)}, u32[]{:S(2)}) %collective-permute-start) | collective-permute-done | bytes 1572896 | tf_op jit(solution)/shard_map/ppermute | solution.py:17
  630.7 13.1 %collective-permute-done.1 = bf16[1,1536,512]{2,1,0:T(8,128)(2,1)} collective-permute-done((bf16[1,1536,512]{2,1,0:T(8,128)(2,1)}, bf16[1,1536,512]{2,1,0:T(8,128)(2,1)}, u32[]{:S(2)}, u32[]{:S(2)}) %collective-permute-start.1) | collective-permute-done | bytes 1572896 | tf_op jit(solution)/shard_map/ppermute | solution.py:17
  643.8 158.1 %all-reduce.3.cloned.1.call-done = (f32[1,2,4,256,256]{3,4,2,1,0:T(8,128)}, f32[1,8,256,256]{3,2,1,0:T(8,128)}, f32[1,8,256,256]{3,2,1,0:T(8,128)}, f32[1,2,4,256,256]{4,3,2,1,0:T(8,128)}) async-done(((f32[1,2,4,256,256]{3,4,2,1,0:T(8,128)}, f32[1,8,256,256]{3,2,1,0:T(8,128)}, f32[1,8,256,256]{3,2,1,0:T(8,128)}, f32[1,2,4,256,256]{4,3,2,1,0:T(8,128)}), (f32[1,2,4,256,256]{3,4,2,1,0:T(8,128)}, ...) | async-done | bytes 8388624 | tf_op jit(solution)/shard_map/psum | solution.py:114
  (99 shorter events, 167.6 us)
Async XLA Ops:
  7.2 253.1 %copy-start = (bf16[1,8,256,256]{3,2,1,0:T(8,128)(2,1)S(1)}, bf16[1,8,256,256]{3,2,1,0:T(8,128)(2,1)}, u32[]{:S(2)}) copy-start(bf16[1,8,256,256]{3,2,1,0:T(8,128)(2,1)} %param.10) | copy-start | bytes 3145732
  9.6 19.6 %copy-start.4 = (bf16[1536,2,256]{2,1,0:T(2,128)(2,1)}, bf16[1536,2,256]{2,1,0:T(2,128)(2,1)S(1)}, u32[]{:S(2)}) copy-start(bf16[1536,2,256]{2,1,0:T(2,128)(2,1)S(1)} %reshape_squeeze.7) | copy-start | bytes 4718596
  44.8 95.7 %all-to-all-start.2 = ((bf16[1536,16,128]{0,2,1:T(8,128)(2,1)}), bf16[1536,16,128]{0,2,1:T(8,128)(2,1)}, u32[]{:S(2)}, u32[]{:S(2)}) async-start(bf16[1536,16,128]{0,2,1:T(8,128)(2,1)} %copy.835), calls=%async_computation.2 | async-start | bytes 12582912 | tf_op jit(solution)/shard_map/all_to_all | solution.py:86
  54.4 19.6 %copy-start.6 = (bf16[1536,2,256]{2,1,0:T(2,128)(2,1)}, bf16[1536,2,256]{2,1,0:T(2,128)(2,1)S(1)}, u32[]{:S(2)}) copy-start(bf16[1536,2,256]{2,1,0:T(2,128)(2,1)S(1)} %reshape_squeeze.6) | copy-start | bytes 4718596
  140.5 100.7 %all-to-all-start = ((bf16[1536,16,128]{0,2,1:T(8,128)(2,1)}), bf16[1536,16,128]{0,2,1:T(8,128)(2,1)}, u32[]{:S(2)}, u32[]{:S(2)}) async-start(bf16[1536,16,128]{0,2,1:T(8,128)(2,1)} %copy.821), calls=%async_computation | async-start | bytes 12582912 | tf_op jit(solution)/shard_map/all_to_all | solution.py:53
  247.4 3.5 copy-start.3
  250.9 9.3 %copy-start.2 = (bf16[1536,8,16,8,2]{0,1,4,3,2:T(8,128)(2,1)}, bf16[1536,8,16,8,2]{0,1,4,3,2:T(8,128)(2,1)S(1)}, u32[]{:S(2)}) copy-start(bf16[1536,8,16,8,2]{0,1,4,3,2:T(8,128)(2,1)S(1)} %copy.823) | copy-start | bytes 18874372
  251.0 19.1 %slice-start = ((s8[6291456]{0:T(1024)(128)(4,1)}), s8[4194304]{0:T(1024)(128)(4,1)S(1)}, s32[]{:S(2)}) async-start(s8[6291456]{0:T(1024)(128)(4,1)} %bitcast.180), calls=%async_computation.5 | async-start | bytes 8388608
  260.2 9.9 %slice-start.1 = ((s8[6291456]{0:T(1024)(128)(4,1)}), s8[2097152]{0:T(1024)(128)(4,1)S(1)}, s32[]{:S(2)}) async-start(s8[6291456]{0:T(1024)(128)(4,1)} %bitcast.180), calls=%async_computation.6 | async-start | bytes 4194304
  344.4 100.8 %all-to-all-start.1 = ((bf16[1536,16,128]{0,2,1:T(8,128)(2,1)}), bf16[1536,16,128]{0,2,1:T(8,128)(2,1)}, u32[]{:S(2)}, u32[]{:S(2)}) async-start(bf16[1536,16,128]{0,2,1:T(8,128)(2,1)} %copy.827), calls=%async_computation.1 | async-start | bytes 12582912 | tf_op jit(solution)/shard_map/all_to_all | solution.py:63
  424.7 18.9 %copy-start.13 = (bf16[1536,1,128]{2,0,1:T(8,128)(2,1)S(1)}, bf16[1536,1,128]{2,0,1:T(8,128)(2,1)}, u32[]{:S(2)}) copy-start(bf16[1536,1,128]{2,0,1:T(8,128)(2,1)} %copy.854) | copy-start | bytes 1179652
  424.7 19.7 %copy-start.12 = (bf16[1536,1,128]{2,0,1:T(8,128)(2,1)S(1)}, bf16[1536,1,128]{2,0,1:T(8,128)(2,1)}, u32[]{:S(2)}) copy-start(bf16[1536,1,128]{2,0,1:T(8,128)(2,1)} %copy.855) | copy-start | bytes 1179652
  426.4 10.2 %copy-start.15 = (bf16[1536,1,128]{2,0,1:T(8,128)(2,1)S(1)}, bf16[1536,1,128]{2,0,1:T(8,128)(2,1)}, u32[]{:S(2)}) copy-start(bf16[1536,1,128]{2,0,1:T(8,128)(2,1)} %copy.849) | copy-start | bytes 1179652
  426.4 11.0 %copy-start.14 = (bf16[1536,1,128]{2,0,1:T(8,128)(2,1)S(1)}, bf16[1536,1,128]{2,0,1:T(8,128)(2,1)}, u32[]{:S(2)}) copy-start(bf16[1536,1,128]{2,0,1:T(8,128)(2,1)} %copy.850) | copy-start | bytes 1179652
  445.2 100.0 %all-to-all-start.3 = ((bf16[16,1536,1,128]{3,1,2,0:T(8,128)(2,1)}), bf16[16,1536,1,128]{3,1,2,0:T(8,128)(2,1)}, u32[]{:S(2)}, u32[]{:S(2)}) async-start(bf16[16,1536,1,128]{3,1,2,0:T(8,128)(2,1)} %bitcast_dynamic-update-slice_fusion), calls=%async_computation.3 | async-start | bytes 12582912 | tf_op jit(solution)/shard_map/all_to_all | solution.py:10
  456.6 345.2 %all-reduce.3.cloned.1.call-start = ((), (), s32[]{:S(2)}) async-start(), calls=%async_computation.4 | async-start | bytes 16777216 | tf_op jit(solution)/shard_map/psum | solution.py:114
  491.3 13.7 %copy-start.5 = (bf16[1536,2,256]{2,1,0:T(2,128)(2,1)S(1)}, bf16[1536,2,256]{2,1,0:T(2,128)(2,1)}, u32[]{:S(2)}) copy-start(bf16[1536,2,256]{2,1,0:T(2,128)(2,1)} %copy-done.4) | copy-start | bytes 4718596
  566.9 13.7 %copy-start.7 = (bf16[1536,2,256]{2,1,0:T(2,128)(2,1)S(1)}, bf16[1536,2,256]{2,1,0:T(2,128)(2,1)}, u32[]{:S(2)}) copy-start(bf16[1536,2,256]{2,1,0:T(2,128)(2,1)} %copy-done.6) | copy-start | bytes 4718596
  586.6 1.2 copy-start.16
  594.0 36.7 %collective-permute-start = (bf16[1,1536,512]{2,1,0:T(8,128)(2,1)}, bf16[1,1536,512]{2,1,0:T(8,128)(2,1)S(1)}, u32[]{:S(2)}, u32[]{:S(2)}) collective-permute-start(bf16[1,1536,512]{2,1,0:T(8,128)(2,1)} %copy.832), channel_id=1, source_target_pairs={{0,16},{16,32},{32,48},{1,17},{17,33},{33,49},{2,18},{18,34},{34,5... | collective-permute-start | bytes 4718600 | tf_op jit(solution)/shard_map/ppermute | solution.py:17
  606.5 37.3 %collective-permute-start.1 = (bf16[1,1536,512]{2,1,0:T(8,128)(2,1)}, bf16[1,1536,512]{2,1,0:T(8,128)(2,1)}, u32[]{:S(2)}, u32[]{:S(2)}) collective-permute-start(bf16[1,1536,512]{2,1,0:T(8,128)(2,1)} %copy.859), channel_id=1, source_target_pairs={{16,0},{32,16},{48,32},{17,1},{33,17},{49,33},{18,2},{34,18},{50,3... | collective-permute-start | bytes 4718600 | tf_op jit(solution)/shard_map/ppermute | solution.py:17
  630.7 13.1 %copy-start.11 = (bf16[1,1536,512]{2,1,0:T(8,128)(2,1)}, bf16[1,1536,512]{2,1,0:T(8,128)(2,1)S(1)}, u32[]{:S(2)}) copy-start(bf16[1,1536,512]{2,1,0:T(8,128)(2,1)S(1)} %collective-permute-done) | copy-start | bytes 4718596
  801.9 8.6 %copy-start.10 = (f32[1,8,256,256]{3,2,1,0:T(8,128)S(1)}, f32[1,8,256,256]{3,2,1,0:T(8,128)}, u32[]{:S(2)}) copy-start(f32[1,8,256,256]{3,2,1,0:T(8,128)} %get-tuple-element.143) | copy-start | bytes 6291460
  804.9 6.9 copy-start.9
  807.7 5.5 copy-start.8
  807.7 6.8 copy-start.1
Sparse Core Ops, SparseCore 0:
  586.7 215.1 all-reduce.2
